TPU v7x, 32 devices: a whole 2x2x4 slice. The times are simulated.
32 devices in a mesh: seq: 4 (over y, core), shard: 8 (over z, x).
Axes of the slice: x: 2, y: 2, z: 4, core: 2. Of those that a mesh axis runs over, the one named last changes fastest.
Arguments:
- tokens: bfloat16 [16384, 768], P(('shard', 'seq')), may hold values from -6 to 6
- doc_lengths: int32 [32], replicated, may hold values from 1 to 1024, 16384 in all
- joint_weight: bfloat16 [768, 2304], P(('seq', 'shard')), may hold values from -0.21875 to 0.21875
- query_bias: bfloat16 [768], P(('seq', 'shard')), may hold values from -3 to 3
- value_bias: bfloat16 [768], P(('seq', 'shard')), may hold values from -3 to 3
- output_weight: bfloat16 [768, 768], P(('seq', 'shard')), may hold values from -1.75 to 1.75
- output_bias: bfloat16 [768], P(('seq', 'shard')), may hold values from -3 to 3
- first_gain: bfloat16 [768], P(('seq', 'shard')), may hold values from 0.5 to 1.5
- first_shift: bfloat16 [768], P(('seq', 'shard')), may hold values from -3 to 3
- inner_weight: bfloat16 [768, 3072], P(('seq', 'shard')), may hold values from -0.21875 to 0.21875
- inner_bias: bfloat16 [3072], P(('seq', 'shard')), may hold values from -3 to 3
- outer_weight: bfloat16 [3072, 768], P(('seq', 'shard')), may hold values from -0.109375 to 0.109375
- outer_bias: bfloat16 [768], P(('seq', 'shard')), may hold values from -3 to 3
- second_gain: bfloat16 [768], P(('seq', 'shard')), may hold values from 0.5 to 1.5
- second_shift: bfloat16 [768], P(('seq', 'shard')), may hold values from -3 to 3
- cotangent: bfloat16 [16384, 768], P(('shard', 'seq')), may hold values from -6 to 6
Outputs:
- layer_out: bfloat16 [16384, 768], P(('shard', 'seq'))
- tokens_grad: float32 [16384, 768], P(('shard', 'seq'))
- joint_weight_grad: float32 [768, 2304], P(('seq', 'shard'))
- query_bias_grad: float32 [768], P(('seq', 'shard'))
- value_bias_grad: float32 [768], P(('seq', 'shard'))
- output_weight_grad: float32 [768, 768], P(('seq', 'shard'))
- output_bias_grad: float32 [768], P(('seq', 'shard'))
- first_gain_grad: float32 [768], P(('seq', 'shard'))
- first_shift_grad: float32 [768], P(('seq', 'shard'))
- inner_weight_grad: float32 [768, 3072], P(('seq', 'shard'))
- inner_bias_grad: float32 [3072], P(('seq', 'shard'))
- outer_weight_grad: float32 [3072, 768], P(('seq', 'shard'))
- outer_bias_grad: float32 [768], P(('seq', 'shard'))
- second_gain_grad: float32 [768], P(('seq', 'shard'))
- second_shift_grad: float32 [768], P(('seq', 'shard'))
Inputs may be any that keep to these rules, and one draw needn't show every extreme that they name: `doc_lengths`: the documents fill the stream in order; running sums of the lengths before each document are its start offset; the longest has exactly 1024 tokens.
All inputs are finite; a program needn't handle non-finite values.
Results may differ from a plain program's by a relative error of at most 0.013.
The roundings to bfloat16 on the way count: a program that leaves them out, or rounds other values in their place, can miss the bound.
Values may be sent and summed in bfloat16 or wider, within the bound.
No kernel may reach another device: no remote copies, remote signals or barrier semaphores. Data moves between devices by JAX's collectives and lax.ppermute only.
A program may use at most 192 MiB of HBM per device.

v0:
```python
import jax
import jax.numpy as jnp
from jax import lax
from jax.sharding import PartitionSpec as P

D = 768
HEADS = 12
HEAD = 64
DOCMAX = 1024
epsilon = 1e-12


def with_halo(cells, sides, width):
    for axis, dim in sides:
        count = lax.axis_size(axis)
        ends = count - 1
        head = lax.slice_in_dim(cells, 0, width, axis=dim)
        tail = lax.slice_in_dim(cells, cells.shape[dim] - width, cells.shape[dim], axis=dim)
        cells = jnp.concatenate(
            [
                lax.ppermute(tail, axis, [(i, (i + 1) % count) for i in range(ends)]),
                cells,
                lax.ppermute(head, axis, [((i + 1) % count, i) for i in range(ends)]),
            ],
            axis=dim,
        )
    return cells


def normalize_keep(value, gain, shift):
    mean = jnp.mean(value, axis=-1, keepdims=True)
    centred = value - mean
    spread = jnp.mean(centred * centred, axis=-1, keepdims=True)
    scale = lax.rsqrt(spread + epsilon)
    normed = centred * scale
    return (normed * gain + shift, normed, scale)


def normalize_back(grad, normed, scale, gain):
    grad_normed = grad * gain
    first = jnp.mean(grad_normed, axis=-1, keepdims=True)
    second = jnp.mean(grad_normed * normed, axis=-1, keepdims=True)
    result = scale * (grad_normed - first - normed * second)
    return (result, jnp.sum(grad * normed, axis=0), jnp.sum(grad, axis=0))


def doc_ids(doc_lengths, positions, total):
    ends = jnp.cumsum(doc_lengths)
    inside = (ends[None, :] <= positions[:, None]).astype(jnp.int32)
    docs = jnp.sum(inside, axis=1)
    valid = (positions >= 0) & (positions < total)
    return jnp.where(valid, docs, -1)


def activate(value):
    return jax.nn.gelu(value, approximate=True)


def left_product(left, right):
    return jnp.einsum("ta,tb->ab", left, right, preferred_element_type=jnp.float32)


def right_product(left, right):
    return jnp.einsum("tb,ab->ta", left, right, preferred_element_type=jnp.float32)


def body(
    tokens,
    doc_lengths,
    joint_weight,
    query_bias,
    value_bias,
    output_weight,
    output_bias,
    first_gain,
    first_shift,
    inner_weight,
    inner_bias,
    outer_weight,
    outer_bias,
    second_gain,
    second_shift,
    cotangent,
):
    seq_count = lax.axis_size("seq")
    shard_count = lax.axis_size("shard")
    rows = tokens.shape[0]
    groups = HEADS // seq_count
    group_width = groups * HEAD
    block = rows * seq_count
    total = block * shard_count
    span_all = block + 2 * DOCMAX
    query_rows = min(512, block)
    count = block // query_rows
    factor = HEAD ** (-0.5)
    params = (
        joint_weight,
        query_bias,
        value_bias,
        output_weight,
        output_bias,
        first_gain,
        first_shift,
        inner_weight,
        inner_bias,
        outer_weight,
        outer_bias,
        second_gain,
        second_shift,
    )
    full = (
        lax.all_gather(params[0], ("seq", "shard"), axis=0, tiled=True),
        lax.all_gather(params[1], ("seq", "shard"), axis=0, tiled=True),
        lax.all_gather(params[2], ("seq", "shard"), axis=0, tiled=True),
        lax.all_gather(params[3], ("seq", "shard"), axis=0, tiled=True),
        lax.all_gather(params[4], ("seq", "shard"), axis=0, tiled=True),
        lax.all_gather(params[5], ("seq", "shard"), axis=0, tiled=True),
        lax.all_gather(params[6], ("seq", "shard"), axis=0, tiled=True),
        lax.all_gather(params[7], ("seq", "shard"), axis=0, tiled=True),
        lax.all_gather(params[8], ("seq", "shard"), axis=0, tiled=True),
        lax.all_gather(params[9], ("seq", "shard"), axis=0, tiled=True),
        lax.all_gather(params[10], ("seq", "shard"), axis=0, tiled=True),
        lax.all_gather(params[11], ("seq", "shard"), axis=0, tiled=True),
        lax.all_gather(params[12], ("seq", "shard"), axis=0, tiled=True),
    )
    (
        joint_full,
        query_full,
        value_full,
        output_full,
        obias_full,
        gain_one,
        shift_one,
        inner_full,
        ibias_full,
        outer_full,
        ubias_full,
        gain_two,
        shift_two,
    ) = full
    base = lax.axis_index("shard") * block
    query_docs = doc_ids(doc_lengths, base + jnp.arange(block, dtype=jnp.int32), total)
    key_docs = doc_ids(doc_lengths, base - DOCMAX + jnp.arange(span_all, dtype=jnp.int32), total)

    def attend_forward(heads_in):
        queries = heads_in[:, 0].reshape(block, groups, HEAD).transpose(1, 0, 2)
        extended = with_halo(heads_in[:, 1:], (("shard", 0),), DOCMAX)
        ext_keys = extended[:, 0].reshape(span_all, groups, HEAD).transpose(1, 0, 2)
        ext_values = extended[:, 1].reshape(span_all, groups, HEAD).transpose(1, 0, 2)

        def scores_of(index):
            query_start = index * query_rows
            query_blk = lax.dynamic_slice_in_dim(queries, query_start, query_rows, 1)
            mask = (
                lax.dynamic_slice_in_dim(query_docs, query_start, query_rows, 0)[:, None]
                == key_docs[None, :]
            )
            scores = (
                jnp.einsum("gqd,gkd->gqk", query_blk, ext_keys, preferred_element_type=jnp.float32)
                * factor
            )
            return (query_blk, ext_keys, ext_values, mask, scores)

        def forward_block(index):
            query_blk, key_blk, value_blk, mask, scores = scores_of(index)
            scores = jnp.where(mask[None], scores, -jnp.inf)
            top = jnp.max(scores, axis=-1, keepdims=True)
            weights = jnp.exp(scores - top)
            summed = jnp.sum(weights, axis=-1, keepdims=True)
            probs = (weights / summed).astype(jnp.bfloat16)
            context = jnp.einsum(
                "gqk,gkd->gqd", probs, value_blk, preferred_element_type=jnp.float32
            )
            return (context.astype(jnp.bfloat16), top + jnp.log(summed))

        ctx_blocks, lse_blocks = lax.map(forward_block, jnp.arange(count, dtype=jnp.int32))
        context_group = ctx_blocks.transpose(0, 2, 1, 3).reshape(block, group_width)
        return (context_group, lse_blocks, scores_of)

    bias_row = jnp.concatenate([query_full, jnp.zeros_like(query_full), value_full]).astype(
        jnp.float32
    )
    joint = (jnp.dot(tokens, joint_full, preferred_element_type=jnp.float32) + bias_row).astype(
        jnp.bfloat16
    )
    heads_in = lax.all_to_all(
        joint.reshape(rows, 3, seq_count, group_width),
        "seq",
        split_axis=2,
        concat_axis=0,
        tiled=True,
    )
    context_group, lse_blocks, scores_of = attend_forward(heads_in.reshape(block, 3, group_width))
    context = context_group.reshape(seq_count, rows, 1, group_width)
    context_tok = lax.all_to_all(context, "seq", split_axis=0, concat_axis=2, tiled=True).reshape(
        rows, D
    )
    attn = jnp.dot(
        context_tok, output_full, preferred_element_type=jnp.float32
    ) + obias_full.astype(jnp.float32)
    hidden, normed_one, scale_one = normalize_keep(
        tokens.astype(jnp.float32) + attn,
        gain_one.astype(jnp.float32),
        shift_one.astype(jnp.float32),
    )
    hidden_low = hidden.astype(jnp.bfloat16)
    inner = jnp.dot(hidden_low, inner_full, preferred_element_type=jnp.float32) + ibias_full.astype(
        jnp.float32
    )
    active, active_back = jax.vjp(activate, inner)
    active_low = active.astype(jnp.bfloat16)
    outer = jnp.dot(active_low, outer_full, preferred_element_type=jnp.float32) + ubias_full.astype(
        jnp.float32
    )
    result, normed_two, scale_two = normalize_keep(
        hidden + outer, gain_two.astype(jnp.float32), shift_two.astype(jnp.float32)
    )
    layer_out = result.astype(jnp.bfloat16)
    grad_two, grad_gain_two, grad_shift_two = normalize_back(
        cotangent.astype(jnp.float32), normed_two, scale_two, gain_two.astype(jnp.float32)
    )
    grad_outer = grad_two.astype(jnp.bfloat16)
    grad_ubias = jnp.sum(grad_outer.astype(jnp.float32), axis=0)
    grad_outer_weight = left_product(active_low, grad_outer)
    grad_active = right_product(grad_outer, outer_full)
    grad_inner = active_back(grad_active)[0].astype(jnp.bfloat16)
    grad_ibias = jnp.sum(grad_inner.astype(jnp.float32), axis=0)
    grad_inner_weight = left_product(hidden_low, grad_inner)
    grad_hidden = grad_two + right_product(grad_inner, inner_full)
    grad_one, grad_gain_one, grad_shift_one = normalize_back(
        grad_hidden, normed_one, scale_one, gain_one.astype(jnp.float32)
    )
    grad_attn = grad_one.astype(jnp.bfloat16)
    grad_obias = jnp.sum(grad_attn.astype(jnp.float32), axis=0)
    grad_output_weight = left_product(context_tok, grad_attn)
    grad_context = right_product(grad_attn, output_full).astype(jnp.bfloat16)
    grad_group = lax.all_to_all(
        grad_context.reshape(1, rows, seq_count, group_width),
        "seq",
        split_axis=2,
        concat_axis=0,
        tiled=True,
    )
    grad_heads = (
        grad_group.reshape(block, group_width).reshape(block, groups, HEAD).transpose(1, 0, 2)
    )

    def backward_block(carry, inputs):
        index, lse = inputs
        query_blk, key_blk, value_blk, mask, scores = scores_of(index)
        probs = jnp.where(mask[None], jnp.exp(scores - lse), 0.0)
        probs_low = probs.astype(jnp.bfloat16)
        grad_blk = lax.dynamic_slice_in_dim(grad_heads, index * query_rows, query_rows, 1)
        grad_probs = jnp.einsum(
            "gqd,gkd->gqk", grad_blk, value_blk, preferred_element_type=jnp.float32
        )
        weighted = jnp.sum(probs * grad_probs, axis=-1, keepdims=True)
        grad_scores = (probs * (grad_probs - weighted)).astype(jnp.bfloat16)
        grad_query = (
            jnp.einsum("gqk,gkd->gqd", grad_scores, key_blk, preferred_element_type=jnp.float32)
            * factor
        )
        grad_key = (
            jnp.einsum("gqk,gqd->gkd", grad_scores, query_blk, preferred_element_type=jnp.float32)
            * factor
        )
        grad_value = jnp.einsum(
            "gqk,gqd->gkd", probs_low, grad_blk, preferred_element_type=jnp.float32
        )
        current = carry
        carry = current + jnp.stack([grad_key, grad_value])
        return (carry, grad_query)

    start_grads = jnp.zeros((2, groups, span_all, HEAD), jnp.float32)
    grad_keyvals, grad_queries = lax.scan(
        backward_block, start_grads, (jnp.arange(count, dtype=jnp.int32), lse_blocks)
    )
    rims = jnp.concatenate(
        [grad_keyvals[:, :, :DOCMAX], grad_keyvals[:, :, DOCMAX + block :]], axis=2
    )
    received = with_halo(rims.astype(jnp.bfloat16), (("shard", 2),), DOCMAX).astype(rims.dtype)
    from_left = received[:, :, :DOCMAX]
    from_right = received[:, :, 3 * DOCMAX :]
    owned = grad_keyvals[:, :, DOCMAX : DOCMAX + block]
    owned = owned.at[:, :, :DOCMAX].add(from_left)
    owned = owned.at[:, :, block - DOCMAX :].add(from_right)
    grad_queries = grad_queries.transpose(1, 0, 2, 3).reshape(groups, block, HEAD)
    stacked = jnp.concatenate([grad_queries[None], owned], axis=0).astype(jnp.bfloat16)
    stacked = stacked.transpose(2, 0, 1, 3).reshape(block, 3, group_width)
    grad_joint = lax.all_to_all(
        stacked.reshape(block, 3, 1, group_width), "seq", split_axis=0, concat_axis=2, tiled=True
    ).reshape(rows, 3 * D)
    grad_joint_weight = left_product(tokens, grad_joint)
    joint_wide = grad_joint.astype(jnp.float32)
    grad_qbias = jnp.sum(joint_wide[:, :D], axis=0)
    grad_vbias = jnp.sum(joint_wide[:, 2 * D :], axis=0)
    tokens_grad = grad_one + right_product(grad_joint, joint_full)
    terms = (
        grad_joint_weight,
        grad_qbias,
        grad_vbias,
        grad_output_weight,
        grad_obias,
        grad_gain_one,
        grad_shift_one,
        grad_inner_weight,
        grad_ibias,
        grad_outer_weight,
        grad_ubias,
        grad_gain_two,
        grad_shift_two,
    )
    reduced = tuple(
        (
            lax.psum_scatter(terms[0], ("seq", "shard"), scatter_dimension=0, tiled=True),
            lax.psum_scatter(terms[1], ("seq", "shard"), scatter_dimension=0, tiled=True),
            lax.psum_scatter(terms[2], ("seq", "shard"), scatter_dimension=0, tiled=True),
            lax.psum_scatter(terms[3], ("seq", "shard"), scatter_dimension=0, tiled=True),
            lax.psum_scatter(terms[4], ("seq", "shard"), scatter_dimension=0, tiled=True),
            lax.psum_scatter(terms[5], ("seq", "shard"), scatter_dimension=0, tiled=True),
            lax.psum_scatter(terms[6], ("seq", "shard"), scatter_dimension=0, tiled=True),
            lax.psum_scatter(terms[7], ("seq", "shard"), scatter_dimension=0, tiled=True),
            lax.psum_scatter(terms[8], ("seq", "shard"), scatter_dimension=0, tiled=True),
            lax.psum_scatter(terms[9], ("seq", "shard"), scatter_dimension=0, tiled=True),
            lax.psum_scatter(terms[10], ("seq", "shard"), scatter_dimension=0, tiled=True),
            lax.psum_scatter(terms[11], ("seq", "shard"), scatter_dimension=0, tiled=True),
            lax.psum_scatter(terms[12], ("seq", "shard"), scatter_dimension=0, tiled=True),
        )
    )
    return (layer_out, tokens_grad) + tuple(reduced)


def solution(mesh):
    placed = (
        P(("shard", "seq"), None),
        P(),
        P(("seq", "shard"), None),
        P(("seq", "shard")),
        P(("seq", "shard")),
        P(("seq", "shard"), None),
        P(("seq", "shard")),
        P(("seq", "shard")),
        P(("seq", "shard")),
        P(("seq", "shard"), None),
        P(("seq", "shard")),
        P(("seq", "shard"), None),
        P(("seq", "shard")),
        P(("seq", "shard")),
        P(("seq", "shard")),
        P(("shard", "seq"), None),
    )
    return jax.shard_map(
        body,
        mesh=mesh,
        in_specs=placed,
        out_specs=(
            P(("shard", "seq"), None),
            P(("shard", "seq"), None),
            P(("seq", "shard"), None),
            P(("seq", "shard")),
            P(("seq", "shard")),
            P(("seq", "shard"), None),
            P(("seq", "shard")),
            P(("seq", "shard")),
            P(("seq", "shard")),
            P(("seq", "shard"), None),
            P(("seq", "shard")),
            P(("seq", "shard"), None),
            P(("seq", "shard")),
            P(("seq", "shard")),
            P(("seq", "shard")),
        ),
        check_vma=False,
    )
```

profile of v0, /device:TPU:0, one launch (start us, length us, event | category | flops | bytes accessed | tf_op | source)
XLA Modules:
  0.0 1033.4 jit_solution(4330060679045575780)
XLA Ops:
  17.0 42.9 %all-reduce.19 = (bf16[768]{0:T(1024)(128)(2,1)S(1)}, bf16[768]{0:T(1024)(128)(2,1)S(1)}, bf16[768]{0:T(1024)(128)(2,1)}, bf16[768]{0:T(1024)(128)(2,1)}, bf16[7...) all-reduce(bf16[768]{0:T(1024)(128)(2,1)S(1)} %dynamic-update-slice, ...), channel_id=1, replica_groups=mesh['seq'=4,'shard'=8] {'seq','shard'}, use_global_device_ids=true, to_apply=%add.1 | all-reduce | flops 9216 | bytes 36864
  59.9 14.2 %all-gather.5.cloned.1.call-done = bf16[768,2304]{1,0:T(8,128)(2,1)} async-done(((bf16[24,2304]{1,0:T(8,128)(2,1)}), bf16[768,2304]{1,0:T(8,128)(2,1)}) %all-gather.5.cloned.1.call-update) | async-done | bytes 3538960 | tf_op jit(solution)/shard_map/all_gather | solution.py:112
  89.0 28.1 %all-to-all-done = bf16[512,3,4,192]{0,3,1,2:T(8,128)(2,1)S(1)} async-done(((bf16[512,3,4,192]{0,3,1,2:T(8,128)(2,1)}), bf16[512,3,4,192]{0,3,1,2:T(8,128)(2,1)S(1)}, u32[]{:S(2)}, u32[]{:S(2)}) %all-to-all-start) | async-done | bytes 2359328 | tf_op jit(solution)/shard_map/all_to_all | solution.py:186
  130.8 32.3 %collective-permute-done = bf16[1024,2,192]{0,2,1:T(8,128)(2,1)S(1)} collective-permute-done((bf16[1024,2,192]{0,2,1:T(8,128)(2,1)S(1)}, bf16[1024,2,192]{0,2,1:T(8,128)(2,1)S(1)}, u32[]{:S(2)}, u32[]{:S(2)}) %collective-permute-start) | collective-permute-done | bytes 786464 | tf_op jit(solution)/shard_map/ppermute | solution.py:21
  165.5 160.2 %while.27 = (s32[]{:T(128)}, bf16[4,3,512,64]{2,3,1,0:T(8,128)(2,1)}, f32[4,3,512,1]{2,1,3,0:T(4,128)S(1)}, s32[4]{0:T(128)S(1)}, s32[2048]{0:T(1024)S(1)}, /*in...) while((s32[]{:T(128)}, ...), condition=%wide.region_6.7_spmd, body=%wide.region_3.6_spmd.sunk | while | flops 1688304128 | bytes 87503056 | solution.py:176
  168.2 12.2 %fusion.113 = (f32[3,512]{1,0:T(4,128)S(1)}, f32[3,512,4096]{2,1,0:T(8,128)}) fusion(pred[512,4096]{1,0:T(8,128)(4,1)S(1)} %broadcast_compare_fusion.4, bf16[3,4096,64]{1,2,0:T(8,128)(2,1)} %get-tuple-element.530, bf16[3,2048,64]{1,2,0:T(8,128)(2,1)S(1)} %get-tuple-element.529, s32[]{:T(128)S(6)} %select_n.67), kind=kOutput, calls=%fused_computation.3.clone.1 | convolution fusion | flops 824179200 | bytes 29038596 | tf_op jit(solution)/shard_map/while/body/eval_jaxpr/gqd,gkd->gqk/dot_general | solution.py:159
  180.4 12.5 %fusion.114 = f32[3,512]{1,0:T(4,128)S(1)} fusion(f32[3,512,4096]{2,1,0:T(8,128)} %get-tuple-element.482, f32[3,512]{1,0:T(4,128)S(1)} %get-tuple-element.483, pred[512,4096]{1,0:T(8,128)(4,1)S(1)} %broadcast_compare_fusion.4), kind=kLoop, calls=%fused_computation.4.clone.1 | loop fusion | flops 25164288 | bytes 27275264 | tf_op jit(solution)/shard_map/while/body/eval_jaxpr/reduce_sum | solution.py:169
  192.9 13.4 %fusion.115 = bf16[4,3,512,64]{2,3,1,0:T(8,128)(2,1)} fusion(bf16[4,3,512,64]{2,3,1,0:T(8,128)(2,1)} %get-tuple-element.511, s32[]{:T(128)S(6)} %copy.102, bf16[3,4096,64]{1,2,0:T(8,128)(2,1)} %get-tuple-element.531, f32[3,512,4096]{2,1,0:T(8,128)} %get-tuple-element.482, f32[3,512]{1,0:T(4,128)S(1)} %fusion.114, ...), kind=kOutput, calls=%fused_computation.9.clone.1 | convolution fusion | flops 836861952 | bytes 29044740 | tf_op jit(solution)/shard_map/while/body/eval_jaxpr/gqk,gkd->gqd/dot_general | solution.py:171
  208.9 12.2 %fusion.113 = (f32[3,512]{1,0:T(4,128)S(1)}, f32[3,512,4096]{2,1,0:T(8,128)}) fusion(pred[512,4096]{1,0:T(8,128)(4,1)S(1)} %broadcast_compare_fusion.4, bf16[3,4096,64]{1,2,0:T(8,128)(2,1)} %get-tuple-element.530, bf16[3,2048,64]{1,2,0:T(8,128)(2,1)S(1)} %get-tuple-element.529, s32[]{:T(128)S(6)} %select_n.67), kind=kOutput, calls=%fused_computation.3.clone.1 | convolution fusion | flops 824179200 | bytes 29038596 | tf_op jit(solution)/shard_map/while/body/eval_jaxpr/gqd,gkd->gqk/dot_general | solution.py:159
  233.0 13.0 %fusion.115 = bf16[4,3,512,64]{2,3,1,0:T(8,128)(2,1)} fusion(bf16[4,3,512,64]{2,3,1,0:T(8,128)(2,1)} %get-tuple-element.511, s32[]{:T(128)S(6)} %copy.102, bf16[3,4096,64]{1,2,0:T(8,128)(2,1)} %get-tuple-element.531, f32[3,512,4096]{2,1,0:T(8,128)} %get-tuple-element.482, f32[3,512]{1,0:T(4,128)S(1)} %fusion.114, ...), kind=kOutput, calls=%fused_computation.9.clone.1 | convolution fusion | flops 836861952 | bytes 29044740 | tf_op jit(solution)/shard_map/while/body/eval_jaxpr/gqk,gkd->gqd/dot_general | solution.py:171
  248.7 12.3 %fusion.113 = (f32[3,512]{1,0:T(4,128)S(1)}, f32[3,512,4096]{2,1,0:T(8,128)}) fusion(pred[512,4096]{1,0:T(8,128)(4,1)S(1)} %broadcast_compare_fusion.4, bf16[3,4096,64]{1,2,0:T(8,128)(2,1)} %get-tuple-element.530, bf16[3,2048,64]{1,2,0:T(8,128)(2,1)S(1)} %get-tuple-element.529, s32[]{:T(128)S(6)} %select_n.67), kind=kOutput, calls=%fused_computation.3.clone.1 | convolution fusion | flops 824179200 | bytes 29038596 | tf_op jit(solution)/shard_map/while/body/eval_jaxpr/gqd,gkd->gqk/dot_general | solution.py:159
  273.0 13.0 %fusion.115 = bf16[4,3,512,64]{2,3,1,0:T(8,128)(2,1)} fusion(bf16[4,3,512,64]{2,3,1,0:T(8,128)(2,1)} %get-tuple-element.511, s32[]{:T(128)S(6)} %copy.102, bf16[3,4096,64]{1,2,0:T(8,128)(2,1)} %get-tuple-element.531, f32[3,512,4096]{2,1,0:T(8,128)} %get-tuple-element.482, f32[3,512]{1,0:T(4,128)S(1)} %fusion.114, ...), kind=kOutput, calls=%fused_computation.9.clone.1 | convolution fusion | flops 836861952 | bytes 29044740 | tf_op jit(solution)/shard_map/while/body/eval_jaxpr/gqk,gkd->gqd/dot_general | solution.py:171
  288.7 12.2 %fusion.113 = (f32[3,512]{1,0:T(4,128)S(1)}, f32[3,512,4096]{2,1,0:T(8,128)}) fusion(pred[512,4096]{1,0:T(8,128)(4,1)S(1)} %broadcast_compare_fusion.4, bf16[3,4096,64]{1,2,0:T(8,128)(2,1)} %get-tuple-element.530, bf16[3,2048,64]{1,2,0:T(8,128)(2,1)S(1)} %get-tuple-element.529, s32[]{:T(128)S(6)} %select_n.67), kind=kOutput, calls=%fused_computation.3.clone.1 | convolution fusion | flops 824179200 | bytes 29038596 | tf_op jit(solution)/shard_map/while/body/eval_jaxpr/gqd,gkd->gqk/dot_general | solution.py:159
  312.7 13.0 %fusion.115 = bf16[4,3,512,64]{2,3,1,0:T(8,128)(2,1)} fusion(bf16[4,3,512,64]{2,3,1,0:T(8,128)(2,1)} %get-tuple-element.511, s32[]{:T(128)S(6)} %copy.102, bf16[3,4096,64]{1,2,0:T(8,128)(2,1)} %get-tuple-element.531, f32[3,512,4096]{2,1,0:T(8,128)} %get-tuple-element.482, f32[3,512]{1,0:T(4,128)S(1)} %fusion.114, ...), kind=kOutput, calls=%fused_computation.9.clone.1 | convolution fusion | flops 836861952 | bytes 29044740 | tf_op jit(solution)/shard_map/while/body/eval_jaxpr/gqk,gkd->gqd/dot_general | solution.py:171
  414.9 362.3 %while.28 = (s32[]{:T(128)}, f32[2,3,4096,64]{2,3,1,0:T(8,128)}, bf16[4,3,512,64]{2,3,1,0:T(8,128)(2,1)}, s32[4]{0:T(128)S(1)}, s32[2048]{0:T(1024)S(1)}, /*inde...) while((s32[]{:T(128)}, f32[2,3,4096,64]{2,3,1,0:T(8,128)}, ...), condition=%wide.region_17.18_spmd.clone, body=%wide.region_15.17_spmd.clone.sunk | while | flops 4128602624 | bytes 284885344 | solution.py:275
  429.6 12.5 %fusion.126 = f32[1,3,4096,64]{2,3,1,0:T(8,128)} fusion(f32[3,512,4096]{2,1,0:T(8,128)} %fusion.125, f32[3,512]{1,0:T(4,128)S(1)} %dynamic-slice_bitcast_fusion.2, pred[512,4096]{1,0:T(8,128)(4,1)S(1)} %broadcast_compare_fusion.5, bf16[3,2048,64]{1,2,0:T(8,128)(2,1)} %get-tuple-element.575, s32[]{:T(128)S(6)} %select_n.71), kind=kOutput, calls=%fused_computation.23.clone.1 | convolution fusion | flops 830472192 | bytes 30611460 | tf_op jit(solution)/shard_map/while/body/eval_jaxpr/gqk,gqd->gkd/dot_general | solution.py:267
  442.1 18.4 %multiply_reduce_fusion.7 = (f32[3,512]{1,0:T(4,128)S(1)}, f32[3,512,4096]{2,1,0:T(8,128)}) fusion(f32[3,512,4096]{2,1,0:T(8,128)} %fusion.125, f32[3,512]{1,0:T(4,128)S(1)} %dynamic-slice_bitcast_fusion.2, pred[512,4096]{1,0:T(8,128)(4,1)S(1)} %broadcast_compare_fusion.5, bf16[3,4096,64]{1,2,0:T(8,128)(2,1)} %get-tuple-element.576, ...), kind=kOutput, calls=%fused_computation.17.clone.1 | convolution fusion | flops 836762112 | bytes 54210564 | tf_op jit(solution)/shard_map/while/body/eval_jaxpr/gqd,gkd->gqk/dot_general | solution.py:254
  460.4 22.0 %multiply_convert_fusion.5 = bf16[3,512,4096]{2,1,0:T(8,128)(2,1)} fusion(f32[3,512,4096]{2,1,0:T(8,128)} %get-tuple-element.495, f32[3,512,4096]{2,1,0:T(8,128)} %fusion.125, f32[3,512]{1,0:T(4,128)S(1)} %get-tuple-element.496, f32[3,512]{1,0:T(4,128)S(1)} %dynamic-slice_bitcast_fusion.2, pred[512,4096]{1,0:T(8,128)(4,1)S(1)} %broadcast_compare_fusion.5), kind=kLoop, calls=%fused_computation.16.clone.1 | loop fusion | flops 37748736 | bytes 65024000 | tf_op jit(solution)/shard_map/while/body/eval_jaxpr/convert_element_type | solution.py:258
  507.1 12.5 %fusion.125 = f32[3,512,4096]{2,1,0:T(8,128)} fusion(bf16[3,4096,64]{1,2,0:T(8,128)(2,1)} %get-tuple-element.573, bf16[3,2048,64]{1,2,0:T(8,128)(2,1)S(1)} %get-tuple-element.572, s32[]{:T(128)S(6)} %select_n.71), kind=kOutput, calls=%fused_computation.34.clone.1 | convolution fusion | flops 805306368 | bytes 26935300 | tf_op jit(solution)/shard_map/while/body/eval_jaxpr/gqd,gkd->gqk/dot_general | solution.py:159
  519.7 13.2 %fusion.126 = f32[1,3,4096,64]{2,3,1,0:T(8,128)} fusion(f32[3,512,4096]{2,1,0:T(8,128)} %fusion.125, f32[3,512]{1,0:T(4,128)S(1)} %dynamic-slice_bitcast_fusion.2, pred[512,4096]{1,0:T(8,128)(4,1)S(1)} %broadcast_compare_fusion.5, bf16[3,2048,64]{1,2,0:T(8,128)(2,1)} %get-tuple-element.575, s32[]{:T(128)S(6)} %select_n.71), kind=kOutput, calls=%fused_computation.23.clone.1 | convolution fusion | flops 830472192 | bytes 30611460 | tf_op jit(solution)/shard_map/while/body/eval_jaxpr/gqk,gqd->gkd/dot_general | solution.py:267
  532.9 19.1 %multiply_reduce_fusion.7 = (f32[3,512]{1,0:T(4,128)S(1)}, f32[3,512,4096]{2,1,0:T(8,128)}) fusion(f32[3,512,4096]{2,1,0:T(8,128)} %fusion.125, f32[3,512]{1,0:T(4,128)S(1)} %dynamic-slice_bitcast_fusion.2, pred[512,4096]{1,0:T(8,128)(4,1)S(1)} %broadcast_compare_fusion.5, bf16[3,4096,64]{1,2,0:T(8,128)(2,1)} %get-tuple-element.576, ...), kind=kOutput, calls=%fused_computation.17.clone.1 | convolution fusion | flops 836762112 | bytes 54210564 | tf_op jit(solution)/shard_map/while/body/eval_jaxpr/gqd,gkd->gqk/dot_general | solution.py:254
  551.9 22.4 %multiply_convert_fusion.5 = bf16[3,512,4096]{2,1,0:T(8,128)(2,1)} fusion(f32[3,512,4096]{2,1,0:T(8,128)} %get-tuple-element.495, f32[3,512,4096]{2,1,0:T(8,128)} %fusion.125, f32[3,512]{1,0:T(4,128)S(1)} %get-tuple-element.496, f32[3,512]{1,0:T(4,128)S(1)} %dynamic-slice_bitcast_fusion.2, pred[512,4096]{1,0:T(8,128)(4,1)S(1)} %broadcast_compare_fusion.5), kind=kLoop, calls=%fused_computation.16.clone.1 | loop fusion | flops 37748736 | bytes 65024000 | tf_op jit(solution)/shard_map/while/body/eval_jaxpr/convert_element_type | solution.py:258
  610.2 12.5 %fusion.126 = f32[1,3,4096,64]{2,3,1,0:T(8,128)} fusion(f32[3,512,4096]{2,1,0:T(8,128)} %fusion.125, f32[3,512]{1,0:T(4,128)S(1)} %dynamic-slice_bitcast_fusion.2, pred[512,4096]{1,0:T(8,128)(4,1)S(1)} %broadcast_compare_fusion.5, bf16[3,2048,64]{1,2,0:T(8,128)(2,1)} %get-tuple-element.575, s32[]{:T(128)S(6)} %select_n.71), kind=kOutput, calls=%fused_computation.23.clone.1 | convolution fusion | flops 830472192 | bytes 30611460 | tf_op jit(solution)/shard_map/while/body/eval_jaxpr/gqk,gqd->gkd/dot_general | solution.py:267
  622.7 18.7 %multiply_reduce_fusion.7 = (f32[3,512]{1,0:T(4,128)S(1)}, f32[3,512,4096]{2,1,0:T(8,128)}) fusion(f32[3,512,4096]{2,1,0:T(8,128)} %fusion.125, f32[3,512]{1,0:T(4,128)S(1)} %dynamic-slice_bitcast_fusion.2, pred[512,4096]{1,0:T(8,128)(4,1)S(1)} %broadcast_compare_fusion.5, bf16[3,4096,64]{1,2,0:T(8,128)(2,1)} %get-tuple-element.576, ...), kind=kOutput, calls=%fused_computation.17.clone.1 | convolution fusion | flops 836762112 | bytes 54210564 | tf_op jit(solution)/shard_map/while/body/eval_jaxpr/gqd,gkd->gqk/dot_general | solution.py:254
  641.4 23.7 %multiply_convert_fusion.5 = bf16[3,512,4096]{2,1,0:T(8,128)(2,1)} fusion(f32[3,512,4096]{2,1,0:T(8,128)} %get-tuple-element.495, f32[3,512,4096]{2,1,0:T(8,128)} %fusion.125, f32[3,512]{1,0:T(4,128)S(1)} %get-tuple-element.496, f32[3,512]{1,0:T(4,128)S(1)} %dynamic-slice_bitcast_fusion.2, pred[512,4096]{1,0:T(8,128)(4,1)S(1)} %broadcast_compare_fusion.5), kind=kLoop, calls=%fused_computation.16.clone.1 | loop fusion | flops 37748736 | bytes 65024000 | tf_op jit(solution)/shard_map/while/body/eval_jaxpr/convert_element_type | solution.py:258
  702.2 12.9 %fusion.126 = f32[1,3,4096,64]{2,3,1,0:T(8,128)} fusion(f32[3,512,4096]{2,1,0:T(8,128)} %fusion.125, f32[3,512]{1,0:T(4,128)S(1)} %dynamic-slice_bitcast_fusion.2, pred[512,4096]{1,0:T(8,128)(4,1)S(1)} %broadcast_compare_fusion.5, bf16[3,2048,64]{1,2,0:T(8,128)(2,1)} %get-tuple-element.575, s32[]{:T(128)S(6)} %select_n.71), kind=kOutput, calls=%fused_computation.23.clone.1 | convolution fusion | flops 830472192 | bytes 30611460 | tf_op jit(solution)/shard_map/while/body/eval_jaxpr/gqk,gqd->gkd/dot_general | solution.py:267
  715.0 18.3 %multiply_reduce_fusion.7 = (f32[3,512]{1,0:T(4,128)S(1)}, f32[3,512,4096]{2,1,0:T(8,128)}) fusion(f32[3,512,4096]{2,1,0:T(8,128)} %fusion.125, f32[3,512]{1,0:T(4,128)S(1)} %dynamic-slice_bitcast_fusion.2, pred[512,4096]{1,0:T(8,128)(4,1)S(1)} %broadcast_compare_fusion.5, bf16[3,4096,64]{1,2,0:T(8,128)(2,1)} %get-tuple-element.576, ...), kind=kOutput, calls=%fused_computation.17.clone.1 | convolution fusion | flops 836762112 | bytes 54210564 | tf_op jit(solution)/shard_map/while/body/eval_jaxpr/gqd,gkd->gqk/dot_general | solution.py:254
  733.3 22.2 %multiply_convert_fusion.5 = bf16[3,512,4096]{2,1,0:T(8,128)(2,1)} fusion(f32[3,512,4096]{2,1,0:T(8,128)} %get-tuple-element.495, f32[3,512,4096]{2,1,0:T(8,128)} %fusion.125, f32[3,512]{1,0:T(4,128)S(1)} %get-tuple-element.496, f32[3,512]{1,0:T(4,128)S(1)} %dynamic-slice_bitcast_fusion.2, pred[512,4096]{1,0:T(8,128)(4,1)S(1)} %broadcast_compare_fusion.5), kind=kLoop, calls=%fused_computation.16.clone.1 | loop fusion | flops 37748736 | bytes 65024000 | tf_op jit(solution)/shard_map/while/body/eval_jaxpr/convert_element_type | solution.py:258
  792.9 27.0 %collective-permute-done.2 = bf16[2,3,1024,64]{2,3,1,0:T(8,128)(2,1)} collective-permute-done((bf16[2,3,1024,64]{2,3,1,0:T(8,128)(2,1)}, bf16[2,3,1024,64]{2,3,1,0:T(8,128)(2,1)}, u32[]{:S(2)}, u32[]{:S(2)}) %collective-permute-start.2) | collective-permute-done | bytes 786464 | tf_op jit(solution)/shard_map/ppermute | solution.py:21
  829.3 53.8 %all_to_all.60 = bf16[2048,3,1,192]{3,1,2,0:T(4,128)(2,1)} all-to-all(bf16[2048,3,1,192]{3,1,2,0:T(4,128)(2,1)} %copy.80), channel_id=1, replica_groups=mesh['seq'=4,'shard'=8] {'seq'}, dimensions={0} | all-to-all | bytes 4718592 | tf_op jit(solution)/shard_map/all_to_all | solution.py:290
  907.3 42.3 %all-reduce.18 = (f32[768]{0:T(1024)S(1)}, f32[768]{0:T(1024)S(1)}, f32[768]{0:T(1024)S(1)}, f32[768]{0:T(1024)S(1)}, f32[768]{0:T(1024)S(1)}, /*index=5*/f32[30...) all-reduce(f32[768]{0:T(1024)S(1)} %get-tuple-element.276, ...), channel_id=3, replica_groups=mesh['seq'=4,'shard'=8] {'seq','shard'}, use_global_device_ids=true, to_apply=%region_20.21.clone | all-reduce | flops 9216 | bytes 73728
  960.5 65.6 %reduce-scatter.13.cloned.1.call-done = f32[24,2304]{1,0:T(8,128)} async-done(((f32[768,2304]{1,0:T(8,128)}), f32[24,2304]{1,0:T(8,128)}) %reduce-scatter.13.cloned.1.call-update) | async-done | bytes 221200
  (283 shorter events, 363.7 us)
Async XLA Ops:
  7.2 66.9 %all-gather.5.cloned.1.call-start = ((), (), s32[]{:S(2)}) async-start(), calls=%async_computation.8 | async-start | bytes 3649536 | tf_op jit(solution)/shard_map/all_gather | solution.py:112
  7.9 321.7 %all-gather.7.cloned.1.call-start = ((), (), s32[]{:S(2)}) async-start(), calls=%async_computation.9 | async-start | bytes 1216512 | tf_op jit(solution)/shard_map/all_gather | solution.py:115
  8.7 336.1 %all-gather.9.cloned.1.call-start = ((), (), s32[]{:S(2)}) async-start(), calls=%async_computation.10 | async-start | bytes 4866048 | tf_op jit(solution)/shard_map/all_gather | solution.py:119
  84.3 32.8 %all-to-all-start = ((bf16[512,3,4,192]{0,3,1,2:T(8,128)(2,1)}), bf16[512,3,4,192]{0,3,1,2:T(8,128)(2,1)S(1)}, u32[]{:S(2)}, u32[]{:S(2)}) async-start(bf16[512,3,4,192]{0,3,1,2:T(8,128)(2,1)} %copy.74), calls=%async_computation | async-start | bytes 4718592 | tf_op jit(solution)/shard_map/all_to_all | solution.py:186
  88.1 263.7 %all-gather.11.cloned.1.call-start = ((), (), s32[]{:S(2)}) async-start(), calls=%async_computation.11 | async-start | bytes 4866048 | tf_op jit(solution)/shard_map/all_gather | solution.py:121
  125.3 37.9 %collective-permute-start = (bf16[1024,2,192]{0,2,1:T(8,128)(2,1)S(1)}, bf16[1024,2,192]{0,2,1:T(8,128)(2,1)S(1)}, u32[]{:S(2)}, u32[]{:S(2)}) collective-permute-start(bf16[1024,2,192]{0,2,1:T(8,128)(2,1)S(1)} %get-tuple-element.355), channel_id=1, source_target_pairs={{0,1},{1,2},{2,3},{3,4},{4,5},{5,6},{6,7},{8,9},{9,10},{10,11},{11... | collective-permute-start | bytes 2359304 | tf_op jit(solution)/shard_map/ppermute | solution.py:21
  128.7 34.5 %collective-permute-start.1 = (bf16[1024,2,192]{0,2,1:T(8,128)(2,1)S(1)}, bf16[1024,2,192]{0,2,1:T(8,128)(2,1)S(1)}, u32[]{:S(2)}, u32[]{:S(2)}) collective-permute-start(bf16[1024,2,192]{0,2,1:T(8,128)(2,1)S(1)} %get-tuple-element.356), channel_id=1, source_target_pairs={{1,0},{2,1},{3,2},{4,3},{5,4},{6,5},{7,6},{9,8},{10,9},{11,10},{12... | collective-permute-start | bytes 2359304 | tf_op jit(solution)/shard_map/ppermute | solution.py:23
  165.5 164.0 %copy-start.25 = (bf16[768]{0:T(1024)(128)(2,1)S(1)}, bf16[768]{0:T(1024)(128)(2,1)}, u32[]{:S(2)}) copy-start(bf16[768]{0:T(1024)(128)(2,1)} %get-tuple-element.339) | copy-start | bytes 4612
  165.5 164.0 %copy-start.24 = (bf16[768]{0:T(1024)(128)(2,1)S(1)}, bf16[768]{0:T(1024)(128)(2,1)}, u32[]{:S(2)}) copy-start(bf16[768]{0:T(1024)(128)(2,1)} %get-tuple-element.338) | copy-start | bytes 4612
  165.5 164.0 %copy-start.23 = (bf16[768]{0:T(1024)(128)(2,1)S(1)}, bf16[768]{0:T(1024)(128)(2,1)}, u32[]{:S(2)}) copy-start(bf16[768]{0:T(1024)(128)(2,1)} %get-tuple-element.342) | copy-start | bytes 4612
  165.5 164.0 %copy-start.22 = (bf16[768]{0:T(1024)(128)(2,1)S(1)}, bf16[768]{0:T(1024)(128)(2,1)}, u32[]{:S(2)}) copy-start(bf16[768]{0:T(1024)(128)(2,1)} %get-tuple-element.336) | copy-start | bytes 4612
  165.5 164.1 %copy-start.21 = (bf16[768]{0:T(1024)(128)(2,1)S(1)}, bf16[768]{0:T(1024)(128)(2,1)}, u32[]{:S(2)}) copy-start(bf16[768]{0:T(1024)(128)(2,1)} %get-tuple-element.337) | copy-start | bytes 4612
  165.5 164.1 %copy-start.20 = (bf16[768]{0:T(1024)(128)(2,1)S(1)}, bf16[768]{0:T(1024)(128)(2,1)}, u32[]{:S(2)}) copy-start(bf16[768]{0:T(1024)(128)(2,1)} %get-tuple-element.341) | copy-start | bytes 4612
  165.5 164.1 %copy-start.17 = (bf16[3072]{0:T(1024)(128)(2,1)S(1)}, bf16[3072]{0:T(1024)(128)(2,1)}, u32[]{:S(2)}) copy-start(bf16[3072]{0:T(1024)(128)(2,1)} %get-tuple-element.340) | copy-start | bytes 18436
  325.7 15.1 %all-to-all-start.1 = ((bf16[4,512,1,192]{1,3,2,0:T(8,128)(2,1)}), bf16[4,512,1,192]{1,3,2,0:T(8,128)(2,1)S(1)}, u32[]{:S(2)}, u32[]{:S(2)}) async-start(bf16[4,512,1,192]{1,3,2,0:T(8,128)(2,1)} %bitcast.14), calls=%async_computation.1 | async-start | bytes 1572864 | tf_op jit(solution)/shard_map/all_to_all | solution.py:195
  329.2 631.2 %reduce-scatter.7.cloned.1.call-start = ((), (), s32[]{:S(2)}) async-start(), calls=%async_computation.12 | async-start | bytes 2433024 | tf_op jit(solution)/shard_map/reduce_scatter | solution.py:318
  351.8 8.1 copy-start.8
  351.8 11.6 %copy-start.28 = (f32[512,3072]{1,0:T(8,128)S(1)}, f32[512,3072]{1,0:T(8,128)}, u32[]{:S(2)}) copy-start(f32[512,3072]{1,0:T(8,128)} %fusion.62) | copy-start | bytes 18874372
  361.2 9.3 slice-start.3
  378.7 581.8 %reduce-scatter.11.cloned.1.call-start = ((), (), s32[]{:S(2)}) async-start(), calls=%async_computation.14 | async-start | bytes 9732096 | tf_op jit(solution)/shard_map/reduce_scatter | solution.py:324
  395.8 15.9 %all-to-all-start.2 = ((bf16[1,512,4,192]{1,3,0,2:T(8,128)(2,1)}), bf16[1,512,4,192]{1,3,0,2:T(8,128)(2,1)}, u32[]{:S(2)}, u32[]{:S(2)}) async-start(bf16[1,512,4,192]{1,3,0,2:T(8,128)(2,1)} %bitcast.132), calls=%async_computation.2 | async-start | bytes 1572864 | tf_op jit(solution)/shard_map/all_to_all | solution.py:237
  400.0 560.5 %reduce-scatter.9.cloned.1.call-start = ((), (), s32[]{:S(2)}) async-start(), calls=%async_computation.13 | async-start | bytes 9732096 | tf_op jit(solution)/shard_map/reduce_scatter | solution.py:322
  407.4 618.8 %reduce-scatter.13.cloned.1.call-start = ((), (), s32[]{:S(2)}) async-start(), calls=%async_computation.15 | async-start | bytes 7299072
  482.4 17.3 %slice-start = ((s8[6291456]{0:T(1024)(128)(4,1)}), s8[2097152]{0:T(1024)(128)(4,1)S(1)}, s32[]{:S(2)}) async-start(s8[6291456]{0:T(1024)(128)(4,1)} %bitcast.118), calls=%async_computation.16 | async-start | bytes 4194304 | tf_op jit(solution)/shard_map/while
  574.3 16.8 %slice-start = ((s8[6291456]{0:T(1024)(128)(4,1)}), s8[2097152]{0:T(1024)(128)(4,1)S(1)}, s32[]{:S(2)}) async-start(s8[6291456]{0:T(1024)(128)(4,1)} %bitcast.118), calls=%async_computation.16 | async-start | bytes 4194304 | tf_op jit(solution)/shard_map/while
  665.1 17.9 %slice-start = ((s8[6291456]{0:T(1024)(128)(4,1)}), s8[2097152]{0:T(1024)(128)(4,1)S(1)}, s32[]{:S(2)}) async-start(s8[6291456]{0:T(1024)(128)(4,1)} %bitcast.118), calls=%async_computation.16 | async-start | bytes 4194304 | tf_op jit(solution)/shard_map/while
  675.1 7.9 slice-start.1
  675.1 7.9 copy-start.2
  755.5 16.9 %slice-start = ((s8[6291456]{0:T(1024)(128)(4,1)}), s8[2097152]{0:T(1024)(128)(4,1)S(1)}, s32[]{:S(2)}) async-start(s8[6291456]{0:T(1024)(128)(4,1)} %bitcast.118), calls=%async_computation.16 | async-start | bytes 4194304 | tf_op jit(solution)/shard_map/while
  777.3 11.0 %copy-start.1 = (f32[2,3,4096,64]{2,3,1,0:T(8,128)S(1)}, f32[2,3,4096,64]{2,3,1,0:T(8,128)}, u32[]{:S(2)}) copy-start(f32[2,3,4096,64]{2,3,1,0:T(8,128)} %get-tuple-element.148) | copy-start | bytes 18874372
  782.0 37.8 %collective-permute-start.2 = (bf16[2,3,1024,64]{2,3,1,0:T(8,128)(2,1)}, bf16[2,3,1024,64]{2,3,1,0:T(8,128)(2,1)}, u32[]{:S(2)}, u32[]{:S(2)}) collective-permute-start(bf16[2,3,1024,64]{2,3,1,0:T(8,128)(2,1)} %get-tuple-element.351), channel_id=1, source_target_pairs={{0,1},{1,2},{2,3},{3,4},{4,5},{5,6},{6,7},{8,9},{9,10},{10,11},{11... | collective-permute-start | bytes 2359304 | tf_op jit(solution)/shard_map/ppermute | solution.py:21
  786.8 33.0 %collective-permute-start.3 = (bf16[2,3,1024,64]{2,3,1,0:T(8,128)(2,1)}, bf16[2,3,1024,64]{2,3,1,0:T(8,128)(2,1)}, u32[]{:S(2)}, u32[]{:S(2)}) collective-permute-start(bf16[2,3,1024,64]{2,3,1,0:T(8,128)(2,1)} %get-tuple-element.352), channel_id=1, source_target_pairs={{1,0},{2,1},{3,2},{4,3},{5,4},{6,5},{7,6},{9,8},{10,9},{11,10},{12... | collective-permute-start | bytes 2359304 | tf_op jit(solution)/shard_map/ppermute | solution.py:23
  (30 other events, 101.7 us)
Sparse Core Ops, SparseCore 0:
  11.0 63.0 all-gather.4
  77.1 53.0 all-gather.6
  133.2 68.0 all-gather.8
  204.0 62.5 all-gather.10
  378.8 98.7 reduce-scatter.6
  484.9 134.7 reduce-scatter.10
  626.2 134.5 reduce-scatter.8
  906.0 120.0 reduce-scatter.12
where the time goes:
time: 1040 us; the launch traced here: 1030 us
  matrix products  412 us (40%)
  waiting for transfers between devices  185 us (18%)
  other arithmetic  171 us (16%)
  blocking collectives  139 us (13%)
  local copies, waits for them, and re-layouts  81 us (8%)
  starting transfers between devices  23.8 us (2%)
  between operations  15.2 us (1%)
    dot_general x8, matrix products, scores_of(): jnp.einsum('gqd,gkd->gqk', query_blk, ext_keys, preferred_element_type=jn...  96.9 us
    convert_element_type x4, other arithmetic, backward_block(): grad_scores = (probs * (grad_probs - weighted)).astype(jnp.bfloat16)  90.3 us
    unnamed x2, blocking collectives  85.2 us
    dot_general x4, matrix products, backward_block(): jnp.einsum('gqd,gkd->gqk', grad_blk, value_blk, preferred_element_type=jn...  74.4 us
    unnamed x9, waiting for transfers between devices  68.3 us
    ppermute x2, waiting for transfers between devices, with_halo(): lax.ppermute(tail, axis, [(i, (i + 1) % count) for i in range(ends)])  59.3 us
    all_to_all x1, blocking collectives, body(): lax.all_to_all(stacked.reshape(block, 3, 1, group_width), 'seq', split_ax...  53.8 us
    dot_general x4, matrix products, forward_block(): jnp.einsum('gqk,gkd->gqd', probs, value_blk, preferred_element_type=jnp.f...  52.5 us
  transfers between devices with their start and end apart: 15, of which 7 were waited for; matrix products, arithmetic and copies ran while one was open for 60% of the time, Pallas kernels for 0%

commit v1 on v0

--- a/solution.py
+++ b/solution.py
@@ -287,8 +287,16 @@
     grad_queries = grad_queries.transpose(1, 0, 2, 3).reshape(groups, block, HEAD)
     stacked = jnp.concatenate([grad_queries[None], owned], axis=0).astype(jnp.bfloat16)
     stacked = stacked.transpose(2, 0, 1, 3).reshape(block, 3, group_width)
-    grad_joint = lax.all_to_all(
-        stacked.reshape(block, 3, 1, group_width), "seq", split_axis=0, concat_axis=2, tiled=True
+    grad_joint = jnp.concatenate(
+        lax.all_to_all(
+            jnp.stack(
+                jnp.split(stacked.reshape(block, 3, 1, group_width), lax.axis_size("seq"), axis=0)
+            ),
+            "seq",
+            0,
+            0,
+        ),
+        axis=2,
     ).reshape(rows, 3 * D)
     grad_joint_weight = left_product(tokens, grad_joint)
     joint_wide = grad_joint.astype(jnp.float32)

time: 1040 us -> 1010 us (0.971)
  blocking collectives: 139 us -> 116 us
  local copies, waits for them, and re-layouts: 81 us -> 68 us
    all_to_all x1, blocking collectives: 53.8 us -> 31 us  [body(): lax.all_to_all(jnp.stack(jnp.split(stacked.reshape(block, 3, 1, group_wid...]
  transfers between devices with their start and end apart: 15 -> 15, of which waited for: 7 -> 7; matrix products, arithmetic and copies ran while one was open for 60% -> 61% of each run, Pallas kernels for 0% -> 0%
where the time goes in v1:
time: 1010 us; the launch traced here: 997 us
  matrix products  412 us (41%)
  waiting for transfers between devices  185 us (18%)
  other arithmetic  171 us (17%)
  blocking collectives  116 us (11%)
  local copies, waits for them, and re-layouts  68 us (7%)
  starting transfers between devices  23.6 us (2%)
  between operations  15 us (1%)
    dot_general x8, matrix products, scores_of(): jnp.einsum('gqd,gkd->gqk', query_blk, ext_keys, preferred_element_type=jn...  96.9 us
    convert_element_type x4, other arithmetic, backward_block(): grad_scores = (probs * (grad_probs - weighted)).astype(jnp.bfloat16)  90.4 us
    unnamed x2, blocking collectives  85.1 us
    dot_general x4, matrix products, backward_block(): jnp.einsum('gqd,gkd->gqk', grad_blk, value_blk, preferred_element_type=jn...  74.3 us
    unnamed x9, waiting for transfers between devices  68.4 us
    ppermute x2, waiting for transfers between devices, with_halo(): lax.ppermute(tail, axis, [(i, (i + 1) % count) for i in range(ends)])  59.5 us
    dot_general x4, matrix products, forward_block(): jnp.einsum('gqk,gkd->gqd', probs, value_blk, preferred_element_type=jnp.f...  52.5 us
    dot_general x4, matrix products, backward_block(): jnp.einsum('gqk,gqd->gkd', probs_low, grad_blk, preferred_element_type=jn...  50.8 us
  transfers between devices with their start and end apart: 15, of which 7 were waited for; matrix products, arithmetic and copies ran while one was open for 61% of the time, Pallas kernels for 0%

profile of v1, /device:TPU:0, one launch (start us, length us, event | category | flops | bytes accessed | tf_op | source)
XLA Modules:
  0.0 997.3 jit_solution(5803356542878531766)
XLA Ops:
  17.0 42.9 %all-reduce.19 = (bf16[768]{0:T(1024)(128)(2,1)S(1)}, bf16[768]{0:T(1024)(128)(2,1)S(1)}, bf16[768]{0:T(1024)(128)(2,1)}, bf16[768]{0:T(1024)(128)(2,1)}, bf16[7...) all-reduce(bf16[768]{0:T(1024)(128)(2,1)S(1)} %dynamic-update-slice, ...), channel_id=1, replica_groups=mesh['seq'=4,'shard'=8] {'seq','shard'}, use_global_device_ids=true, to_apply=%add.1 | all-reduce | flops 9216 | bytes 36864
  59.9 14.2 %all-gather.5.cloned.1.call-done = bf16[768,2304]{1,0:T(8,128)(2,1)} async-done(((bf16[24,2304]{1,0:T(8,128)(2,1)}), bf16[768,2304]{1,0:T(8,128)(2,1)}) %all-gather.5.cloned.1.call-update) | async-done | bytes 3538960 | tf_op jit(solution)/shard_map/all_gather | solution.py:112
  89.0 28.1 %all-to-all-done = bf16[512,3,4,192]{0,3,1,2:T(8,128)(2,1)S(1)} async-done(((bf16[512,3,4,192]{0,3,1,2:T(8,128)(2,1)}), bf16[512,3,4,192]{0,3,1,2:T(8,128)(2,1)S(1)}, u32[]{:S(2)}, u32[]{:S(2)}) %all-to-all-start) | async-done | bytes 2359328 | tf_op jit(solution)/shard_map/all_to_all | solution.py:186
  130.7 32.6 %collective-permute-done = bf16[1024,2,192]{0,2,1:T(8,128)(2,1)S(1)} collective-permute-done((bf16[1024,2,192]{0,2,1:T(8,128)(2,1)S(1)}, bf16[1024,2,192]{0,2,1:T(8,128)(2,1)S(1)}, u32[]{:S(2)}, u32[]{:S(2)}) %collective-permute-start) | collective-permute-done | bytes 786464 | tf_op jit(solution)/shard_map/ppermute | solution.py:21
  165.6 160.2 %while.27 = (s32[]{:T(128)}, bf16[4,3,512,64]{2,3,1,0:T(8,128)(2,1)}, f32[4,3,512,1]{2,1,3,0:T(4,128)S(1)}, s32[4]{0:T(128)S(1)}, s32[2048]{0:T(1024)S(1)}, /*in...) while((s32[]{:T(128)}, ...), condition=%wide.region_6.7_spmd, body=%wide.region_3.6_spmd.sunk | while | flops 1688304128 | bytes 87503056 | solution.py:176
  168.2 12.2 %fusion.114 = (f32[3,512]{1,0:T(4,128)S(1)}, f32[3,512,4096]{2,1,0:T(8,128)}) fusion(pred[512,4096]{1,0:T(8,128)(4,1)S(1)} %broadcast_compare_fusion.4, bf16[3,4096,64]{1,2,0:T(8,128)(2,1)} %get-tuple-element.519, bf16[3,2048,64]{1,2,0:T(8,128)(2,1)S(1)} %get-tuple-element.518, s32[]{:T(128)S(6)} %select_n.67), kind=kOutput, calls=%fused_computation.3.clone.1 | convolution fusion | flops 824179200 | bytes 29038596 | tf_op jit(solution)/shard_map/while/body/eval_jaxpr/gqd,gkd->gqk/dot_general | solution.py:159
  180.4 12.5 %fusion.115 = f32[3,512]{1,0:T(4,128)S(1)} fusion(f32[3,512,4096]{2,1,0:T(8,128)} %get-tuple-element.471, f32[3,512]{1,0:T(4,128)S(1)} %get-tuple-element.472, pred[512,4096]{1,0:T(8,128)(4,1)S(1)} %broadcast_compare_fusion.4), kind=kLoop, calls=%fused_computation.4.clone.1 | loop fusion | flops 25164288 | bytes 27275264 | tf_op jit(solution)/shard_map/while/body/eval_jaxpr/reduce_sum | solution.py:169
  192.9 13.4 %fusion.116 = bf16[4,3,512,64]{2,3,1,0:T(8,128)(2,1)} fusion(bf16[4,3,512,64]{2,3,1,0:T(8,128)(2,1)} %get-tuple-element.500, s32[]{:T(128)S(6)} %copy.84, bf16[3,4096,64]{1,2,0:T(8,128)(2,1)} %get-tuple-element.520, f32[3,512,4096]{2,1,0:T(8,128)} %get-tuple-element.471, f32[3,512]{1,0:T(4,128)S(1)} %fusion.115, ...), kind=kOutput, calls=%fused_computation.9.clone.1 | convolution fusion | flops 836861952 | bytes 29044740 | tf_op jit(solution)/shard_map/while/body/eval_jaxpr/gqk,gkd->gqd/dot_general | solution.py:171
  209.0 12.2 %fusion.114 = (f32[3,512]{1,0:T(4,128)S(1)}, f32[3,512,4096]{2,1,0:T(8,128)}) fusion(pred[512,4096]{1,0:T(8,128)(4,1)S(1)} %broadcast_compare_fusion.4, bf16[3,4096,64]{1,2,0:T(8,128)(2,1)} %get-tuple-element.519, bf16[3,2048,64]{1,2,0:T(8,128)(2,1)S(1)} %get-tuple-element.518, s32[]{:T(128)S(6)} %select_n.67), kind=kOutput, calls=%fused_computation.3.clone.1 | convolution fusion | flops 824179200 | bytes 29038596 | tf_op jit(solution)/shard_map/while/body/eval_jaxpr/gqd,gkd->gqk/dot_general | solution.py:159
  233.0 13.1 %fusion.116 = bf16[4,3,512,64]{2,3,1,0:T(8,128)(2,1)} fusion(bf16[4,3,512,64]{2,3,1,0:T(8,128)(2,1)} %get-tuple-element.500, s32[]{:T(128)S(6)} %copy.84, bf16[3,4096,64]{1,2,0:T(8,128)(2,1)} %get-tuple-element.520, f32[3,512,4096]{2,1,0:T(8,128)} %get-tuple-element.471, f32[3,512]{1,0:T(4,128)S(1)} %fusion.115, ...), kind=kOutput, calls=%fused_computation.9.clone.1 | convolution fusion | flops 836861952 | bytes 29044740 | tf_op jit(solution)/shard_map/while/body/eval_jaxpr/gqk,gkd->gqd/dot_general | solution.py:171
  248.7 12.3 %fusion.114 = (f32[3,512]{1,0:T(4,128)S(1)}, f32[3,512,4096]{2,1,0:T(8,128)}) fusion(pred[512,4096]{1,0:T(8,128)(4,1)S(1)} %broadcast_compare_fusion.4, bf16[3,4096,64]{1,2,0:T(8,128)(2,1)} %get-tuple-element.519, bf16[3,2048,64]{1,2,0:T(8,128)(2,1)S(1)} %get-tuple-element.518, s32[]{:T(128)S(6)} %select_n.67), kind=kOutput, calls=%fused_computation.3.clone.1 | convolution fusion | flops 824179200 | bytes 29038596 | tf_op jit(solution)/shard_map/while/body/eval_jaxpr/gqd,gkd->gqk/dot_general | solution.py:159
  273.0 13.0 %fusion.116 = bf16[4,3,512,64]{2,3,1,0:T(8,128)(2,1)} fusion(bf16[4,3,512,64]{2,3,1,0:T(8,128)(2,1)} %get-tuple-element.500, s32[]{:T(128)S(6)} %copy.84, bf16[3,4096,64]{1,2,0:T(8,128)(2,1)} %get-tuple-element.520, f32[3,512,4096]{2,1,0:T(8,128)} %get-tuple-element.471, f32[3,512]{1,0:T(4,128)S(1)} %fusion.115, ...), kind=kOutput, calls=%fused_computation.9.clone.1 | convolution fusion | flops 836861952 | bytes 29044740 | tf_op jit(solution)/shard_map/while/body/eval_jaxpr/gqk,gkd->gqd/dot_general | solution.py:171
  288.7 12.2 %fusion.114 = (f32[3,512]{1,0:T(4,128)S(1)}, f32[3,512,4096]{2,1,0:T(8,128)}) fusion(pred[512,4096]{1,0:T(8,128)(4,1)S(1)} %broadcast_compare_fusion.4, bf16[3,4096,64]{1,2,0:T(8,128)(2,1)} %get-tuple-element.519, bf16[3,2048,64]{1,2,0:T(8,128)(2,1)S(1)} %get-tuple-element.518, s32[]{:T(128)S(6)} %select_n.67), kind=kOutput, calls=%fused_computation.3.clone.1 | convolution fusion | flops 824179200 | bytes 29038596 | tf_op jit(solution)/shard_map/while/body/eval_jaxpr/gqd,gkd->gqk/dot_general | solution.py:159
  312.7 13.0 %fusion.116 = bf16[4,3,512,64]{2,3,1,0:T(8,128)(2,1)} fusion(bf16[4,3,512,64]{2,3,1,0:T(8,128)(2,1)} %get-tuple-element.500, s32[]{:T(128)S(6)} %copy.84, bf16[3,4096,64]{1,2,0:T(8,128)(2,1)} %get-tuple-element.520, f32[3,512,4096]{2,1,0:T(8,128)} %get-tuple-element.471, f32[3,512]{1,0:T(4,128)S(1)} %fusion.115, ...), kind=kOutput, calls=%fused_computation.9.clone.1 | convolution fusion | flops 836861952 | bytes 29044740 | tf_op jit(solution)/shard_map/while/body/eval_jaxpr/gqk,gkd->gqd/dot_general | solution.py:171
  414.7 362.3 %while.28 = (s32[]{:T(128)}, f32[2,3,4096,64]{2,3,1,0:T(8,128)}, bf16[4,3,512,64]{2,3,1,0:T(8,128)(2,1)}, s32[4]{0:T(128)S(1)}, s32[2048]{0:T(1024)S(1)}, /*inde...) while((s32[]{:T(128)}, f32[2,3,4096,64]{2,3,1,0:T(8,128)}, ...), condition=%wide.region_17.18_spmd.clone, body=%wide.region_15.17_spmd.clone.sunk | while | flops 4128602624 | bytes 284885344 | solution.py:275
  429.4 12.4 %fusion.127 = f32[1,3,4096,64]{2,3,1,0:T(8,128)} fusion(f32[3,512,4096]{2,1,0:T(8,128)} %fusion.126, f32[3,512]{1,0:T(4,128)S(1)} %dynamic-slice_bitcast_fusion.2, pred[512,4096]{1,0:T(8,128)(4,1)S(1)} %broadcast_compare_fusion.5, bf16[3,2048,64]{1,2,0:T(8,128)(2,1)} %get-tuple-element.564, s32[]{:T(128)S(6)} %select_n.71), kind=kOutput, calls=%fused_computation.23.clone.1 | convolution fusion | flops 830472192 | bytes 30611460 | tf_op jit(solution)/shard_map/while/body/eval_jaxpr/gqk,gqd->gkd/dot_general | solution.py:267
  441.8 18.3 %multiply_reduce_fusion.7 = (f32[3,512]{1,0:T(4,128)S(1)}, f32[3,512,4096]{2,1,0:T(8,128)}) fusion(f32[3,512,4096]{2,1,0:T(8,128)} %fusion.126, f32[3,512]{1,0:T(4,128)S(1)} %dynamic-slice_bitcast_fusion.2, pred[512,4096]{1,0:T(8,128)(4,1)S(1)} %broadcast_compare_fusion.5, bf16[3,4096,64]{1,2,0:T(8,128)(2,1)} %get-tuple-element.565, ...), kind=kOutput, calls=%fused_computation.17.clone.1 | convolution fusion | flops 836762112 | bytes 54210564 | tf_op jit(solution)/shard_map/while/body/eval_jaxpr/gqd,gkd->gqk/dot_general | solution.py:254
  460.1 22.0 %multiply_convert_fusion.5 = bf16[3,512,4096]{2,1,0:T(8,128)(2,1)} fusion(f32[3,512,4096]{2,1,0:T(8,128)} %get-tuple-element.484, f32[3,512,4096]{2,1,0:T(8,128)} %fusion.126, f32[3,512]{1,0:T(4,128)S(1)} %get-tuple-element.485, f32[3,512]{1,0:T(4,128)S(1)} %dynamic-slice_bitcast_fusion.2, pred[512,4096]{1,0:T(8,128)(4,1)S(1)} %broadcast_compare_fusion.5), kind=kLoop, calls=%fused_computation.16.clone.1 | loop fusion | flops 37748736 | bytes 65024000 | tf_op jit(solution)/shard_map/while/body/eval_jaxpr/convert_element_type | solution.py:258
  506.8 12.5 %fusion.126 = f32[3,512,4096]{2,1,0:T(8,128)} fusion(bf16[3,4096,64]{1,2,0:T(8,128)(2,1)} %get-tuple-element.562, bf16[3,2048,64]{1,2,0:T(8,128)(2,1)S(1)} %get-tuple-element.561, s32[]{:T(128)S(6)} %select_n.71), kind=kOutput, calls=%fused_computation.34.clone.1 | convolution fusion | flops 805306368 | bytes 26935300 | tf_op jit(solution)/shard_map/while/body/eval_jaxpr/gqd,gkd->gqk/dot_general | solution.py:159
  519.3 13.2 %fusion.127 = f32[1,3,4096,64]{2,3,1,0:T(8,128)} fusion(f32[3,512,4096]{2,1,0:T(8,128)} %fusion.126, f32[3,512]{1,0:T(4,128)S(1)} %dynamic-slice_bitcast_fusion.2, pred[512,4096]{1,0:T(8,128)(4,1)S(1)} %broadcast_compare_fusion.5, bf16[3,2048,64]{1,2,0:T(8,128)(2,1)} %get-tuple-element.564, s32[]{:T(128)S(6)} %select_n.71), kind=kOutput, calls=%fused_computation.23.clone.1 | convolution fusion | flops 830472192 | bytes 30611460 | tf_op jit(solution)/shard_map/while/body/eval_jaxpr/gqk,gqd->gkd/dot_general | solution.py:267
  532.5 19.1 %multiply_reduce_fusion.7 = (f32[3,512]{1,0:T(4,128)S(1)}, f32[3,512,4096]{2,1,0:T(8,128)}) fusion(f32[3,512,4096]{2,1,0:T(8,128)} %fusion.126, f32[3,512]{1,0:T(4,128)S(1)} %dynamic-slice_bitcast_fusion.2, pred[512,4096]{1,0:T(8,128)(4,1)S(1)} %broadcast_compare_fusion.5, bf16[3,4096,64]{1,2,0:T(8,128)(2,1)} %get-tuple-element.565, ...), kind=kOutput, calls=%fused_computation.17.clone.1 | convolution fusion | flops 836762112 | bytes 54210564 | tf_op jit(solution)/shard_map/while/body/eval_jaxpr/gqd,gkd->gqk/dot_general | solution.py:254
  551.6 22.3 %multiply_convert_fusion.5 = bf16[3,512,4096]{2,1,0:T(8,128)(2,1)} fusion(f32[3,512,4096]{2,1,0:T(8,128)} %get-tuple-element.484, f32[3,512,4096]{2,1,0:T(8,128)} %fusion.126, f32[3,512]{1,0:T(4,128)S(1)} %get-tuple-element.485, f32[3,512]{1,0:T(4,128)S(1)} %dynamic-slice_bitcast_fusion.2, pred[512,4096]{1,0:T(8,128)(4,1)S(1)} %broadcast_compare_fusion.5), kind=kLoop, calls=%fused_computation.16.clone.1 | loop fusion | flops 37748736 | bytes 65024000 | tf_op jit(solution)/shard_map/while/body/eval_jaxpr/convert_element_type | solution.py:258
  609.8 12.4 %fusion.127 = f32[1,3,4096,64]{2,3,1,0:T(8,128)} fusion(f32[3,512,4096]{2,1,0:T(8,128)} %fusion.126, f32[3,512]{1,0:T(4,128)S(1)} %dynamic-slice_bitcast_fusion.2, pred[512,4096]{1,0:T(8,128)(4,1)S(1)} %broadcast_compare_fusion.5, bf16[3,2048,64]{1,2,0:T(8,128)(2,1)} %get-tuple-element.564, s32[]{:T(128)S(6)} %select_n.71), kind=kOutput, calls=%fused_computation.23.clone.1 | convolution fusion | flops 830472192 | bytes 30611460 | tf_op jit(solution)/shard_map/while/body/eval_jaxpr/gqk,gqd->gkd/dot_general | solution.py:267
  622.2 18.7 %multiply_reduce_fusion.7 = (f32[3,512]{1,0:T(4,128)S(1)}, f32[3,512,4096]{2,1,0:T(8,128)}) fusion(f32[3,512,4096]{2,1,0:T(8,128)} %fusion.126, f32[3,512]{1,0:T(4,128)S(1)} %dynamic-slice_bitcast_fusion.2, pred[512,4096]{1,0:T(8,128)(4,1)S(1)} %broadcast_compare_fusion.5, bf16[3,4096,64]{1,2,0:T(8,128)(2,1)} %get-tuple-element.565, ...), kind=kOutput, calls=%fused_computation.17.clone.1 | convolution fusion | flops 836762112 | bytes 54210564 | tf_op jit(solution)/shard_map/while/body/eval_jaxpr/gqd,gkd->gqk/dot_general | solution.py:254
  640.9 23.6 %multiply_convert_fusion.5 = bf16[3,512,4096]{2,1,0:T(8,128)(2,1)} fusion(f32[3,512,4096]{2,1,0:T(8,128)} %get-tuple-element.484, f32[3,512,4096]{2,1,0:T(8,128)} %fusion.126, f32[3,512]{1,0:T(4,128)S(1)} %get-tuple-element.485, f32[3,512]{1,0:T(4,128)S(1)} %dynamic-slice_bitcast_fusion.2, pred[512,4096]{1,0:T(8,128)(4,1)S(1)} %broadcast_compare_fusion.5), kind=kLoop, calls=%fused_computation.16.clone.1 | loop fusion | flops 37748736 | bytes 65024000 | tf_op jit(solution)/shard_map/while/body/eval_jaxpr/convert_element_type | solution.py:258
  701.7 12.8 %fusion.127 = f32[1,3,4096,64]{2,3,1,0:T(8,128)} fusion(f32[3,512,4096]{2,1,0:T(8,128)} %fusion.126, f32[3,512]{1,0:T(4,128)S(1)} %dynamic-slice_bitcast_fusion.2, pred[512,4096]{1,0:T(8,128)(4,1)S(1)} %broadcast_compare_fusion.5, bf16[3,2048,64]{1,2,0:T(8,128)(2,1)} %get-tuple-element.564, s32[]{:T(128)S(6)} %select_n.71), kind=kOutput, calls=%fused_computation.23.clone.1 | convolution fusion | flops 830472192 | bytes 30611460 | tf_op jit(solution)/shard_map/while/body/eval_jaxpr/gqk,gqd->gkd/dot_general | solution.py:267
  714.4 18.3 %multiply_reduce_fusion.7 = (f32[3,512]{1,0:T(4,128)S(1)}, f32[3,512,4096]{2,1,0:T(8,128)}) fusion(f32[3,512,4096]{2,1,0:T(8,128)} %fusion.126, f32[3,512]{1,0:T(4,128)S(1)} %dynamic-slice_bitcast_fusion.2, pred[512,4096]{1,0:T(8,128)(4,1)S(1)} %broadcast_compare_fusion.5, bf16[3,4096,64]{1,2,0:T(8,128)(2,1)} %get-tuple-element.565, ...), kind=kOutput, calls=%fused_computation.17.clone.1 | convolution fusion | flops 836762112 | bytes 54210564 | tf_op jit(solution)/shard_map/while/body/eval_jaxpr/gqd,gkd->gqk/dot_general | solution.py:254
  732.7 22.4 %multiply_convert_fusion.5 = bf16[3,512,4096]{2,1,0:T(8,128)(2,1)} fusion(f32[3,512,4096]{2,1,0:T(8,128)} %get-tuple-element.484, f32[3,512,4096]{2,1,0:T(8,128)} %fusion.126, f32[3,512]{1,0:T(4,128)S(1)} %get-tuple-element.485, f32[3,512]{1,0:T(4,128)S(1)} %dynamic-slice_bitcast_fusion.2, pred[512,4096]{1,0:T(8,128)(4,1)S(1)} %broadcast_compare_fusion.5), kind=kLoop, calls=%fused_computation.16.clone.1 | loop fusion | flops 37748736 | bytes 65024000 | tf_op jit(solution)/shard_map/while/body/eval_jaxpr/convert_element_type | solution.py:258
  792.6 27.0 %collective-permute-done.2 = bf16[2,3,1024,64]{2,3,1,0:T(8,128)(2,1)} collective-permute-done((bf16[2,3,1024,64]{2,3,1,0:T(8,128)(2,1)}, bf16[2,3,1024,64]{2,3,1,0:T(8,128)(2,1)}, u32[]{:S(2)}, u32[]{:S(2)}) %collective-permute-start.2) | collective-permute-done | bytes 786464 | tf_op jit(solution)/shard_map/ppermute | solution.py:21
  825.0 31.0 %all_to_all.50 = bf16[4,512,3,1,192]{1,4,2,3,0:T(8,128)(2,1)S(1)} all-to-all(bf16[4,512,3,1,192]{1,4,2,3,0:T(8,128)(2,1)S(1)} %pad_maximum_fusion.1), channel_id=1, replica_groups=mesh['seq'=4,'shard'=8] {'seq'}, dimensions={0} | all-to-all | bytes 4718592 | tf_op jit(solution)/shard_map/all_to_all | solution.py:291
  871.5 42.2 %all-reduce.18 = (f32[768]{0:T(1024)S(1)}, f32[768]{0:T(1024)S(1)}, f32[768]{0:T(1024)S(1)}, f32[768]{0:T(1024)S(1)}, f32[768]{0:T(1024)S(1)}, /*index=5*/f32[30...) all-reduce(f32[768]{0:T(1024)S(1)} %get-tuple-element.261, ...), channel_id=3, replica_groups=mesh['seq'=4,'shard'=8] {'seq','shard'}, use_global_device_ids=true, to_apply=%region_20.21.clone | all-reduce | flops 9216 | bytes 73728
  924.6 65.8 %reduce-scatter.13.cloned.1.call-done = f32[24,2304]{1,0:T(8,128)} async-done(((f32[768,2304]{1,0:T(8,128)}), f32[24,2304]{1,0:T(8,128)}) %reduce-scatter.13.cloned.1.call-update) | async-done | bytes 221200
  (283 shorter events, 350.6 us)
Async XLA Ops:
  7.2 66.9 %all-gather.5.cloned.1.call-start = ((), (), s32[]{:S(2)}) async-start(), calls=%async_computation.8 | async-start | bytes 3649536 | tf_op jit(solution)/shard_map/all_gather | solution.py:112
  7.9 322.0 %all-gather.7.cloned.1.call-start = ((), (), s32[]{:S(2)}) async-start(), calls=%async_computation.9 | async-start | bytes 1216512 | tf_op jit(solution)/shard_map/all_gather | solution.py:115
  8.7 336.1 %all-gather.9.cloned.1.call-start = ((), (), s32[]{:S(2)}) async-start(), calls=%async_computation.10 | async-start | bytes 4866048 | tf_op jit(solution)/shard_map/all_gather | solution.py:119
  84.3 32.8 %all-to-all-start = ((bf16[512,3,4,192]{0,3,1,2:T(8,128)(2,1)}), bf16[512,3,4,192]{0,3,1,2:T(8,128)(2,1)S(1)}, u32[]{:S(2)}, u32[]{:S(2)}) async-start(bf16[512,3,4,192]{0,3,1,2:T(8,128)(2,1)} %copy.59), calls=%async_computation | async-start | bytes 4718592 | tf_op jit(solution)/shard_map/all_to_all | solution.py:186
  88.1 263.7 %all-gather.11.cloned.1.call-start = ((), (), s32[]{:S(2)}) async-start(), calls=%async_computation.11 | async-start | bytes 4866048 | tf_op jit(solution)/shard_map/all_gather | solution.py:121
  125.3 37.9 %collective-permute-start = (bf16[1024,2,192]{0,2,1:T(8,128)(2,1)S(1)}, bf16[1024,2,192]{0,2,1:T(8,128)(2,1)S(1)}, u32[]{:S(2)}, u32[]{:S(2)}) collective-permute-start(bf16[1024,2,192]{0,2,1:T(8,128)(2,1)S(1)} %get-tuple-element.344), channel_id=1, source_target_pairs={{0,1},{1,2},{2,3},{3,4},{4,5},{5,6},{6,7},{8,9},{9,10},{10,11},{11... | collective-permute-start | bytes 2359304 | tf_op jit(solution)/shard_map/ppermute | solution.py:21
  128.7 34.5 %collective-permute-start.1 = (bf16[1024,2,192]{0,2,1:T(8,128)(2,1)S(1)}, bf16[1024,2,192]{0,2,1:T(8,128)(2,1)S(1)}, u32[]{:S(2)}, u32[]{:S(2)}) collective-permute-start(bf16[1024,2,192]{0,2,1:T(8,128)(2,1)S(1)} %get-tuple-element.345), channel_id=1, source_target_pairs={{1,0},{2,1},{3,2},{4,3},{5,4},{6,5},{7,6},{9,8},{10,9},{11,10},{12... | collective-permute-start | bytes 2359304 | tf_op jit(solution)/shard_map/ppermute | solution.py:23
  165.5 164.3 %copy-start.25 = (bf16[768]{0:T(1024)(128)(2,1)S(1)}, bf16[768]{0:T(1024)(128)(2,1)}, u32[]{:S(2)}) copy-start(bf16[768]{0:T(1024)(128)(2,1)} %get-tuple-element.324) | copy-start | bytes 4612
  165.5 164.3 %copy-start.24 = (bf16[768]{0:T(1024)(128)(2,1)S(1)}, bf16[768]{0:T(1024)(128)(2,1)}, u32[]{:S(2)}) copy-start(bf16[768]{0:T(1024)(128)(2,1)} %get-tuple-element.323) | copy-start | bytes 4612
  165.5 164.3 %copy-start.23 = (bf16[768]{0:T(1024)(128)(2,1)S(1)}, bf16[768]{0:T(1024)(128)(2,1)}, u32[]{:S(2)}) copy-start(bf16[768]{0:T(1024)(128)(2,1)} %get-tuple-element.327) | copy-start | bytes 4612
  165.5 164.3 %copy-start.22 = (bf16[768]{0:T(1024)(128)(2,1)S(1)}, bf16[768]{0:T(1024)(128)(2,1)}, u32[]{:S(2)}) copy-start(bf16[768]{0:T(1024)(128)(2,1)} %get-tuple-element.321) | copy-start | bytes 4612
  165.5 164.3 %copy-start.21 = (bf16[768]{0:T(1024)(128)(2,1)S(1)}, bf16[768]{0:T(1024)(128)(2,1)}, u32[]{:S(2)}) copy-start(bf16[768]{0:T(1024)(128)(2,1)} %get-tuple-element.322) | copy-start | bytes 4612
  165.6 164.3 %copy-start.20 = (bf16[768]{0:T(1024)(128)(2,1)S(1)}, bf16[768]{0:T(1024)(128)(2,1)}, u32[]{:S(2)}) copy-start(bf16[768]{0:T(1024)(128)(2,1)} %get-tuple-element.326) | copy-start | bytes 4612
  165.6 164.3 %copy-start.17 = (bf16[3072]{0:T(1024)(128)(2,1)S(1)}, bf16[3072]{0:T(1024)(128)(2,1)}, u32[]{:S(2)}) copy-start(bf16[3072]{0:T(1024)(128)(2,1)} %get-tuple-element.325) | copy-start | bytes 18436
  325.7 15.1 %all-to-all-start.1 = ((bf16[4,512,1,192]{1,3,2,0:T(8,128)(2,1)}), bf16[4,512,1,192]{1,3,2,0:T(8,128)(2,1)S(1)}, u32[]{:S(2)}, u32[]{:S(2)}) async-start(bf16[4,512,1,192]{1,3,2,0:T(8,128)(2,1)} %bitcast.14), calls=%async_computation.1 | async-start | bytes 1572864 | tf_op jit(solution)/shard_map/all_to_all | solution.py:195
  329.3 595.3 %reduce-scatter.7.cloned.1.call-start = ((), (), s32[]{:S(2)}) async-start(), calls=%async_computation.12 | async-start | bytes 2433024 | tf_op jit(solution)/shard_map/reduce_scatter | solution.py:326
  351.8 8.1 copy-start.8
  351.8 11.5 %copy-start.28 = (f32[512,3072]{1,0:T(8,128)S(1)}, f32[512,3072]{1,0:T(8,128)}, u32[]{:S(2)}) copy-start(f32[512,3072]{1,0:T(8,128)} %fusion.62) | copy-start | bytes 18874372
  361.2 9.3 slice-start.3
  378.7 545.9 %reduce-scatter.11.cloned.1.call-start = ((), (), s32[]{:S(2)}) async-start(), calls=%async_computation.14 | async-start | bytes 9732096 | tf_op jit(solution)/shard_map/reduce_scatter | solution.py:332
  395.5 15.9 %all-to-all-start.2 = ((bf16[1,512,4,192]{1,3,0,2:T(8,128)(2,1)}), bf16[1,512,4,192]{1,3,0,2:T(8,128)(2,1)}, u32[]{:S(2)}, u32[]{:S(2)}) async-start(bf16[1,512,4,192]{1,3,0,2:T(8,128)(2,1)} %bitcast.132), calls=%async_computation.2 | async-start | bytes 1572864 | tf_op jit(solution)/shard_map/all_to_all | solution.py:237
  399.7 524.9 %reduce-scatter.9.cloned.1.call-start = ((), (), s32[]{:S(2)}) async-start(), calls=%async_computation.13 | async-start | bytes 9732096 | tf_op jit(solution)/shard_map/reduce_scatter | solution.py:330
  407.2 583.2 %reduce-scatter.13.cloned.1.call-start = ((), (), s32[]{:S(2)}) async-start(), calls=%async_computation.15 | async-start | bytes 7299072
  482.1 17.3 %slice-start = ((s8[6291456]{0:T(1024)(128)(4,1)}), s8[2097152]{0:T(1024)(128)(4,1)S(1)}, s32[]{:S(2)}) async-start(s8[6291456]{0:T(1024)(128)(4,1)} %bitcast.121), calls=%async_computation.16 | async-start | bytes 4194304 | tf_op jit(solution)/shard_map/while
  573.9 16.8 %slice-start = ((s8[6291456]{0:T(1024)(128)(4,1)}), s8[2097152]{0:T(1024)(128)(4,1)S(1)}, s32[]{:S(2)}) async-start(s8[6291456]{0:T(1024)(128)(4,1)} %bitcast.121), calls=%async_computation.16 | async-start | bytes 4194304 | tf_op jit(solution)/shard_map/while
  664.5 17.9 %slice-start = ((s8[6291456]{0:T(1024)(128)(4,1)}), s8[2097152]{0:T(1024)(128)(4,1)S(1)}, s32[]{:S(2)}) async-start(s8[6291456]{0:T(1024)(128)(4,1)} %bitcast.121), calls=%async_computation.16 | async-start | bytes 4194304 | tf_op jit(solution)/shard_map/while
  674.6 7.9 slice-start.1
  674.6 7.9 copy-start.2
  755.1 16.9 %slice-start = ((s8[6291456]{0:T(1024)(128)(4,1)}), s8[2097152]{0:T(1024)(128)(4,1)S(1)}, s32[]{:S(2)}) async-start(s8[6291456]{0:T(1024)(128)(4,1)} %bitcast.121), calls=%async_computation.16 | async-start | bytes 4194304 | tf_op jit(solution)/shard_map/while
  777.1 11.0 %copy-start.1 = (f32[2,3,4096,64]{2,3,1,0:T(8,128)S(1)}, f32[2,3,4096,64]{2,3,1,0:T(8,128)}, u32[]{:S(2)}) copy-start(f32[2,3,4096,64]{2,3,1,0:T(8,128)} %get-tuple-element.148) | copy-start | bytes 18874372
  781.7 37.9 %collective-permute-start.2 = (bf16[2,3,1024,64]{2,3,1,0:T(8,128)(2,1)}, bf16[2,3,1024,64]{2,3,1,0:T(8,128)(2,1)}, u32[]{:S(2)}, u32[]{:S(2)}) collective-permute-start(bf16[2,3,1024,64]{2,3,1,0:T(8,128)(2,1)} %get-tuple-element.336), channel_id=1, source_target_pairs={{0,1},{1,2},{2,3},{3,4},{4,5},{5,6},{6,7},{8,9},{9,10},{10,11},{11... | collective-permute-start | bytes 2359304 | tf_op jit(solution)/shard_map/ppermute | solution.py:21
  786.6 33.0 %collective-permute-start.3 = (bf16[2,3,1024,64]{2,3,1,0:T(8,128)(2,1)}, bf16[2,3,1024,64]{2,3,1,0:T(8,128)(2,1)}, u32[]{:S(2)}, u32[]{:S(2)}) collective-permute-start(bf16[2,3,1024,64]{2,3,1,0:T(8,128)(2,1)} %get-tuple-element.337), channel_id=1, source_target_pairs={{1,0},{2,1},{3,2},{4,3},{5,4},{6,5},{7,6},{9,8},{10,9},{11,10},{12... | collective-permute-start | bytes 2359304 | tf_op jit(solution)/shard_map/ppermute | solution.py:23
  (30 other events, 100.5 us)
Sparse Core Ops, SparseCore 0:
  11.0 63.0 all-gather.4
  77.1 53.0 all-gather.6
  133.2 68.0 all-gather.8
  204.1 62.4 all-gather.10
  378.8 98.7 reduce-scatter.6
  484.9 134.3 reduce-scatter.10
  625.8 134.8 reduce-scatter.8
  870.2 120.1 reduce-scatter.12
